TPU v7x, 32 devices: a whole 2x2x4 slice. The times are simulated.
32 devices in a mesh: seq: 8 (over z, y), tp: 4 (over x, core).
Axes of the slice: x: 2, y: 2, z: 4, core: 2. Of those that a mesh axis runs over, the one named last changes fastest.
Arguments:
- states: bfloat16 [2048, 1536], P('seq', 'tp')
- modulation: float32 [3, 1536], replicated, may hold values from -2.5 to 2.5
- query_weight: bfloat16 [1536, 1536], P(None, 'tp')
- key_weight: bfloat16 [1536, 1536], P(None, 'tp')
- value_weight: bfloat16 [1536, 1536], P(None, 'tp'), may hold values from -0.15625 to 0.15625
- out_weight: bfloat16 [1536, 1536], P(None, 'tp'), may hold values from -0.15625 to 0.15625
- pattern: int32 [16, 7], replicated, may hold values from 0 to 15, as said below
Outputs:
- updated: bfloat16 [2048, 1536], P('seq', 'tp')
Inputs may be any that keep to these rules, and one draw needn't show every extreme that they name: `pattern`: the 2 query tiles 2 d to 2 d + 1 list the same set of 7 distinct tiles, each in an order of its own: all tiles 2 d to 2 d + 1, and exactly one tile from each of 5 other groups of 2 tiles (group e being tiles 2 e to 2 e + 1).
All inputs are finite; a program needn't handle non-finite values.
Results may differ from a plain program's by a relative error of at most 0.0056.
Values may be sent and summed in bfloat16 or wider, within the bound.
A program may use at most 128 MiB of HBM per device.

v0:
```python
import math
import jax
import jax.numpy as jnp
from jax import lax
from jax.sharding import PartitionSpec as P

HD = 128
TILE = 128


def local(states, modulation, query_weight, key_weight, value_weight, out_weight, pattern):
    tok_rows, local_cols = states.shape
    col_start = lax.axis_index("tp") * local_cols
    mod_cols = lax.dynamic_slice_in_dim(modulation, col_start, local_cols, 1)
    states_f = states.astype(jnp.float32)
    gathered = lax.all_gather(states, "tp", axis=1, tiled=True)
    gathered_f = gathered.astype(jnp.float32)
    row_mean = jnp.mean(gathered_f, axis=1, keepdims=True)
    centered = gathered_f - row_mean
    variance = jnp.mean(centered * centered, axis=1, keepdims=True)
    normed = (
        centered * lax.rsqrt(variance + 1e-06) * (1.0 + modulation[1]) + modulation[0]
    ).astype(jnp.bfloat16)
    query = jnp.dot(normed, query_weight, preferred_element_type=jnp.float32).astype(jnp.bfloat16)
    keys = jnp.dot(normed, key_weight, preferred_element_type=jnp.float32).astype(jnp.bfloat16)
    values = jnp.dot(normed, value_weight, preferred_element_type=jnp.float32).astype(jnp.bfloat16)
    head_cols = query.shape[1]
    heads_local = head_cols // HD
    key_value = jnp.concatenate([keys, values], axis=1)
    tiles_dev = tok_rows // TILE
    devices = lax.axis_size("seq")
    seq_index = lax.axis_index("seq")
    list_count = pattern.shape[1]
    groups = pattern.reshape(devices, tiles_dev, list_count)
    first_lists = groups[:, 0, :]
    my_list = lax.dynamic_index_in_dim(first_lists, seq_index, 0, keepdims=False)
    all_tiles = lax.all_gather(key_value, "seq", axis=0, tiled=True)
    tile_store = all_tiles.reshape(devices * tiles_dev, TILE, 2 * head_cols)
    listed_rows = jnp.take(tile_store, my_list, axis=0).reshape(
        list_count * TILE, 2, heads_local, HD
    )
    key_rows = listed_rows[:, 0]
    value_rows = listed_rows[:, 1]
    factor = 1.0 / math.sqrt(HD)
    block_rows = min(512, tok_rows)
    block_count = tok_rows // block_rows

    def attend(query_block):
        scores = (
            jnp.einsum("qhd,khd->hqk", query_block, key_rows, preferred_element_type=jnp.float32)
            * factor
        )
        row_max = jnp.max(scores, axis=2, keepdims=True)
        weights_full = jnp.exp(scores - row_max)
        weight_sum = jnp.sum(weights_full, axis=2)
        weights = weights_full.astype(jnp.bfloat16)
        summed = jnp.einsum("hqk,khd->qhd", weights, value_rows, preferred_element_type=jnp.float32)
        return (summed / jnp.transpose(weight_sum)[:, :, None]).astype(jnp.bfloat16)

    query_blocks = query.reshape(block_count, block_rows, heads_local, HD)
    attended = lax.map(attend, query_blocks).reshape(tok_rows, head_cols)
    projected = jnp.dot(
        lax.all_gather(attended, "tp", axis=1, tiled=True),
        out_weight,
        preferred_element_type=jnp.float32,
    )
    return (states_f + mod_cols[2] * projected).astype(jnp.bfloat16)


def solution(mesh):
    placed = (P("seq", "tp"), P(), P(None, "tp"), P(None, "tp"), P(None, "tp"), P(None, "tp"), P())
    return jax.shard_map(
        local, mesh=mesh, in_specs=placed, out_specs=P("seq", "tp"), check_vma=False
    )
```

profile of v0, /device:TPU:0, one launch (start us, length us, event | category | flops | bytes accessed | tf_op | source)
XLA Modules:
  0.0 108.7 jit_solution(18333908711656933639)
XLA Ops:
  6.5 0.0 copy-start
  6.5 0.0 all-gather.2.cloned.1.call-start
  6.5 0.9 add_reduce_fusion
  7.4 10.3 %all_gather.9 = bf16[256,1536]{1,0:T(8,128)(2,1)S(1)} all-gather(bf16[256,384]{1,0:T(8,128)(2,1)} %param.7), channel_id=1, replica_groups=mesh['seq'=8,'tp'=4] {'tp'}, dimensions={1}, use_global_device_ids=true | all-gather | bytes 983040 | tf_op jit(solution)/shard_map/all_gather | solution.py:16
  17.7 0.2 convert_reduce_fusion
  17.9 0.3 fusion.4
  18.3 0.0 copy-done
  18.3 0.0 copy-start.3
  18.3 0.6 convolution_convert_fusion.1
  18.9 0.6 copy-done.3
  19.6 0.6 convolution_convert_fusion.2
  20.2 0.8 pad_maximum_fusion
  21.0 0.0 all-gather.2.cloned.1.call-update
  21.0 0.0 copy-done.2
  21.0 0.1 copy.16
  21.1 0.0 copy-done.4
  21.1 0.7 convolution_convert_fusion
  21.8 0.1 copy.19
  21.9 0.8 dynamic-slice_reduce_fusion
  22.7 0.1 broadcast_bitcast_fusion
  22.8 59.2 %all-gather.2.cloned.1.call-done = bf16[2048,768]{1,0:T(8,128)(2,1)} async-done(((bf16[256,768]{1,0:T(8,128)(2,1)}), bf16[2048,768]{1,0:T(8,128)(2,1)}) %all-gather.2.cloned.1.call-update) | async-done | bytes 3145744 | tf_op jit(solution)/shard_map/all_gather | solution.py:37
  82.0 3.6 %gather_fusion = bf16[7,128,768]{2,1,0:T(8,128)(2,1)} fusion(bf16[16,128,768]{2,1,0:T(8,128)(2,1)} %bitcast.34, s32[1024]{0:T(1024)S(1)} %pad_clamp_fusion), kind=kCustom, calls=%fused_computation | custom fusion | bytes 2752540 | tf_op jit(solution)/shard_map/jit(_take)/gather | solution.py:39
  85.6 3.9 %reshape.76 = bf16[896,2,3,128]{3,2,1,0:T(4,128)(2,1)S(1)} reshape(bf16[7,128,768]{2,1,0:T(8,128)(2,1)} %gather_fusion) | data formatting | bytes 2752512 | tf_op jit(solution)/shard_map/jit(_take)/gather | solution.py:39
  89.5 0.3 copy_select_fusion
  89.8 0.7 multiply_reduce_fusion
  90.5 0.7 fusion
  91.1 0.0 copy-start.5
  91.1 0.8 fusion.19
  92.0 8.6 %all_gather.11 = bf16[256,1536]{0,1:T(8,128)(2,1)S(1)} all-gather(bf16[256,384]{0,1:T(8,128)(2,1)S(1)} %bitcast.35), channel_id=1, replica_groups=mesh['seq'=8,'tp'=4] {'tp'}, dimensions={1}, use_global_device_ids=true | all-gather | bytes 983040 | tf_op jit(solution)/shard_map/all_gather | solution.py:63
  100.5 0.0 copy-done.1
  100.5 0.0 copy-done.5
  100.5 1.3 %fusion.22 = bf16[256,384]{1,0:T(8,128)(2,1)} fusion(bf16[256,1536]{0,1:T(8,128)(2,1)S(1)} %all_gather.11, bf16[1536,384]{1,0:T(8,128)(2,1)S(1)} %copy-done.5, bf16[256,384]{1,0:T(8,128)(2,1)S(1)} %copy-done.1, f32[384]{0:T(512)S(1)} %dynamic-slice_reduce_fusion), kind=kOutput, calls=%fused_computation.25 | convolution fusion | flops 302383104 | bytes 2360832 | tf_op jit(solution)/shard_map/dot_general | solution.py:62
  (9 shorter events, 0.0 us)
Async XLA Ops:
  6.5 11.7 %copy-start = (bf16[1536,384]{1,0:T(8,128)(2,1)S(1)}, bf16[1536,384]{1,0:T(8,128)(2,1)}, u32[]{:S(2)}) copy-start(bf16[1536,384]{1,0:T(8,128)(2,1)} %param.11) | copy-start | bytes 3538948
  6.5 75.5 %all-gather.2.cloned.1.call-start = ((), (), s32[]{:S(2)}) async-start(), calls=%async_computation | async-start | bytes 3538944 | tf_op jit(solution)/shard_map/all_gather | solution.py:37
  18.3 1.3 %copy-start.3 = (bf16[1536,384]{1,0:T(8,128)(2,1)S(1)}, bf16[1536,384]{1,0:T(8,128)(2,1)}, u32[]{:S(2)}) copy-start(bf16[1536,384]{1,0:T(8,128)(2,1)} %param.10) | copy-start | bytes 3538948
  19.6 1.4 %copy-start.2 = (s32[16,7]{0,1:T(8,128)S(1)}, s32[16,7]{0,1:T(8,128)}, u32[]{:S(2)}) copy-start(s32[16,7]{0,1:T(8,128)} %param.13) | copy-start | bytes 1348
  19.6 1.5 %copy-start.4 = (bf16[1536,384]{1,0:T(8,128)(2,1)S(1)}, bf16[1536,384]{1,0:T(8,128)(2,1)}, u32[]{:S(2)}) copy-start(bf16[1536,384]{1,0:T(8,128)(2,1)} %param.9) | copy-start | bytes 3538948
  91.1 9.4 %copy-start.1 = (bf16[256,384]{1,0:T(8,128)(2,1)S(1)}, bf16[256,384]{1,0:T(8,128)(2,1)}, u32[]{:S(2)}) copy-start(bf16[256,384]{1,0:T(8,128)(2,1)} %param.7) | copy-start | bytes 589828
  91.1 9.4 %copy-start.5 = (bf16[1536,384]{1,0:T(8,128)(2,1)S(1)}, bf16[1536,384]{1,0:T(8,128)(2,1)}, u32[]{:S(2)}) copy-start(bf16[1536,384]{1,0:T(8,128)(2,1)} %param.12) | copy-start | bytes 3538948
Sparse Core Ops, SparseCore 0:
  21.1 60.8 all-gather.1
where the time goes:
time: 109 us
  waiting for transfers between devices  59.2 us (54%)
  blocking collectives  18.9 us (17%)
  between operations  13.5 us (12%)
  local copies, waits for them, and re-layouts  9.24 us (8%)
  matrix products  4.7 us (4%)
  other arithmetic  3.14 us (3%)
    all_gather x1, waiting for transfers between devices, local(): all_tiles = lax.all_gather(key_value, 'seq', axis=0, tiled=True)  59.2 us
    all_gather x1, blocking collectives, local(): gathered = lax.all_gather(states, 'tp', axis=1, tiled=True)  10.3 us
    all_gather x1, blocking collectives, local(): lax.all_gather(attended, 'tp', axis=1, tiled=True)  8.58 us
    gather x2, local copies, waits for them, and re-layouts, local(): jnp.take(tile_store, my_list, axis=0)  7.5 us
  transfers between devices with their start and end apart: 1, of which 1 were waited for; matrix products, arithmetic and copies ran while one was open for 2% of the time, Pallas kernels for 0%

commit v1 on v0

--- a/solution.py
+++ b/solution.py
@@ -60,7 +60,9 @@
     query_blocks = query.reshape(block_count, block_rows, heads_local, HD)
     attended = lax.map(attend, query_blocks).reshape(tok_rows, head_cols)
     projected = jnp.dot(
-        lax.all_gather(attended, "tp", axis=1, tiled=True),
+        jnp.concatenate(
+            lax.all_to_all(jnp.stack([attended] * lax.axis_size("tp")), "tp", 0, 0), axis=1
+        ),
         out_weight,
         preferred_element_type=jnp.float32,
     )

time: 109 us -> 116 us (1.064)
  waiting for transfers between devices: 59.2 us -> 70.8 us
  blocking collectives: 18.9 us -> 10.3 us
  starting transfers between devices: 0.01 us -> 3.49 us
    all_to_all x0 -> x1, waiting for transfers between devices: none -> 10.8 us  [local(): lax.all_to_all(jnp.stack([attended] * lax.axis_size('tp')), 'tp', 0, 0)]
    all_gather x1 -> x0, blocking collectives: 8.58 us -> none  [local(): lax.all_gather(attended, 'tp', axis=1, tiled=True)]
    all_to_all x0 -> x1, starting transfers between devices: none -> 3.49 us  [local(): lax.all_to_all(jnp.stack([attended] * lax.axis_size('tp')), 'tp', 0, 0)]
  transfers between devices with their start and end apart: 1 -> 2, of which waited for: 1 -> 2; matrix products, arithmetic and copies ran while one was open for 2% -> 2% of each run, Pallas kernels for 0% -> 0%
where the time goes in v1:
time: 116 us
  waiting for transfers between devices  70.8 us (61%)
  between operations  13.5 us (12%)
  blocking collectives  10.3 us (9%)
  local copies, waits for them, and re-layouts  10.2 us (9%)
  matrix products  4.71 us (4%)
  starting transfers between devices  3.49 us (3%)
  other arithmetic  3.15 us (3%)
    all_gather x1, waiting for transfers between devices, local(): all_tiles = lax.all_gather(key_value, 'seq', axis=0, tiled=True)  60 us
    all_to_all x1, waiting for transfers between devices, local(): lax.all_to_all(jnp.stack([attended] * lax.axis_size('tp')), 'tp', 0, 0)  10.8 us
    all_gather x1, blocking collectives, local(): gathered = lax.all_gather(states, 'tp', axis=1, tiled=True)  10.3 us
    gather x2, local copies, waits for them, and re-layouts, local(): jnp.take(tile_store, my_list, axis=0)  7.5 us
    all_to_all x1, starting transfers between devices, local(): lax.all_to_all(jnp.stack([attended] * lax.axis_size('tp')), 'tp', 0, 0)  3.49 us
  transfers between devices with their start and end apart: 2, of which 2 were waited for; matrix products, arithmetic and copies ran while one was open for 2% of the time, Pallas kernels for 0%

profile of v1, /device:TPU:0, one launch (start us, length us, event | category | flops | bytes accessed | tf_op | source)
XLA Modules:
  0.0 116.1 jit_solution(8941184287464039428)
XLA Ops:
  6.5 0.0 copy-start
  6.5 0.0 all-gather.2.cloned.1.call-start
  6.5 0.9 add_reduce_fusion
  7.4 10.3 %all_gather.6 = bf16[256,1536]{1,0:T(8,128)(2,1)S(1)} all-gather(bf16[256,384]{1,0:T(8,128)(2,1)} %param.7), channel_id=1, replica_groups=mesh['seq'=8,'tp'=4] {'tp'}, dimensions={1}, use_global_device_ids=true | all-gather | bytes 983040 | tf_op jit(solution)/shard_map/all_gather | solution.py:16
  17.7 0.2 convert_reduce_fusion
  17.9 0.3 fusion.4
  18.3 0.0 copy-done
  18.3 0.0 copy-start.3
  18.3 0.6 convolution_convert_fusion.1
  18.9 0.6 copy-done.3
  19.6 0.6 convolution_convert_fusion.2
  20.2 0.8 pad_maximum_fusion
  21.0 0.0 all-gather.2.cloned.1.call-update
  21.0 0.1 copy.17
  21.1 0.7 convolution_convert_fusion
  21.8 0.1 copy.20
  22.0 0.1 broadcast_bitcast_fusion
  22.0 60.0 %all-gather.2.cloned.1.call-done = bf16[2048,768]{1,0:T(8,128)(2,1)} async-done(((bf16[256,768]{1,0:T(8,128)(2,1)}), bf16[2048,768]{1,0:T(8,128)(2,1)}) %all-gather.2.cloned.1.call-update) | async-done | bytes 3145744 | tf_op jit(solution)/shard_map/all_gather | solution.py:37
  82.0 3.6 %gather_fusion = bf16[7,128,768]{2,1,0:T(8,128)(2,1)} fusion(bf16[16,128,768]{2,1,0:T(8,128)(2,1)} %bitcast.38, s32[1024]{0:T(1024)S(1)} %pad_clamp_fusion), kind=kCustom, calls=%fused_computation | custom fusion | bytes 2752540 | tf_op jit(solution)/shard_map/jit(_take)/gather | solution.py:39
  85.6 3.9 %reshape.82 = bf16[896,2,3,128]{3,2,1,0:T(4,128)(2,1)S(1)} reshape(bf16[7,128,768]{2,1,0:T(8,128)(2,1)} %gather_fusion) | data formatting | bytes 2752512 | tf_op jit(solution)/shard_map/jit(_take)/gather | solution.py:39
  89.5 0.3 copy_select_fusion
  89.8 0.7 multiply_reduce_fusion
  90.5 0.7 fusion
  91.1 0.8 fusion.19
  91.9 0.0 copy-start.1
  91.9 0.0 copy-start.5
  92.0 0.9 stack.3
  92.9 3.5 %all-to-all-start = ((bf16[4,256,384]{1,2,0:T(8,128)(2,1)}), bf16[4,256,384]{1,2,0:T(8,128)(2,1)S(1)}, u32[]{:S(2)}, u32[]{:S(2)}) async-start(bf16[4,256,384]{1,2,0:T(8,128)(2,1)} %stack.3), calls=%async_computation | async-start | bytes 1572864 | tf_op jit(solution)/shard_map/all_to_all | solution.py:64
  96.4 0.8 dynamic-slice_reduce_fusion
  97.2 10.8 %all-to-all-done = bf16[4,256,384]{1,2,0:T(8,128)(2,1)S(1)} async-done(((bf16[4,256,384]{1,2,0:T(8,128)(2,1)}), bf16[4,256,384]{1,2,0:T(8,128)(2,1)S(1)}, u32[]{:S(2)}, u32[]{:S(2)}) %all-to-all-start) | async-done | bytes 786464 | tf_op jit(solution)/shard_map/all_to_all | solution.py:64
  108.0 0.0 copy-done.1
  108.0 1.3 %fusion.22 = bf16[256,384]{1,0:T(8,128)(2,1)} fusion(bf16[256,1536]{0,1:T(8,128)(2,1)S(1)} %bitcast.37, bf16[1536,384]{1,0:T(8,128)(2,1)S(1)} %copy-done.5, bf16[256,384]{1,0:T(8,128)(2,1)S(1)} %copy-done.1, f32[384]{0:T(512)S(1)} %dynamic-slice_reduce_fusion), kind=kOutput, calls=%fused_computation.25 | convolution fusion | flops 302383104 | bytes 2360832 | tf_op jit(solution)/shard_map/dot_general | solution.py:62
  (11 shorter events, 0.1 us)
Async XLA Ops:
  6.5 11.7 %copy-start = (bf16[1536,384]{1,0:T(8,128)(2,1)S(1)}, bf16[1536,384]{1,0:T(8,128)(2,1)}, u32[]{:S(2)}) copy-start(bf16[1536,384]{1,0:T(8,128)(2,1)} %param.11) | copy-start | bytes 3538948
  6.5 75.5 %all-gather.2.cloned.1.call-start = ((), (), s32[]{:S(2)}) async-start(), calls=%async_computation.1 | async-start | bytes 3538944 | tf_op jit(solution)/shard_map/all_gather | solution.py:37
  18.3 1.3 %copy-start.3 = (bf16[1536,384]{1,0:T(8,128)(2,1)S(1)}, bf16[1536,384]{1,0:T(8,128)(2,1)}, u32[]{:S(2)}) copy-start(bf16[1536,384]{1,0:T(8,128)(2,1)} %param.10) | copy-start | bytes 3538948
  19.6 1.4 %copy-start.2 = (s32[16,7]{0,1:T(8,128)S(1)}, s32[16,7]{0,1:T(8,128)}, u32[]{:S(2)}) copy-start(s32[16,7]{0,1:T(8,128)} %param.13) | copy-start | bytes 1348
  19.6 1.5 %copy-start.4 = (bf16[1536,384]{1,0:T(8,128)(2,1)S(1)}, bf16[1536,384]{1,0:T(8,128)(2,1)}, u32[]{:S(2)}) copy-start(bf16[1536,384]{1,0:T(8,128)(2,1)} %param.9) | copy-start | bytes 3538948
  91.9 16.0 %copy-start.1 = (bf16[256,384]{1,0:T(8,128)(2,1)S(1)}, bf16[256,384]{1,0:T(8,128)(2,1)}, u32[]{:S(2)}) copy-start(bf16[256,384]{1,0:T(8,128)(2,1)} %param.7) | copy-start | bytes 589828
  91.9 16.0 %copy-start.5 = (bf16[1536,384]{1,0:T(8,128)(2,1)S(1)}, bf16[1536,384]{1,0:T(8,128)(2,1)}, u32[]{:S(2)}) copy-start(bf16[1536,384]{1,0:T(8,128)(2,1)} %param.12) | copy-start | bytes 3538948
  92.9 15.1 %all-to-all-start = ((bf16[4,256,384]{1,2,0:T(8,128)(2,1)}), bf16[4,256,384]{1,2,0:T(8,128)(2,1)S(1)}, u32[]{:S(2)}, u32[]{:S(2)}) async-start(bf16[4,256,384]{1,2,0:T(8,128)(2,1)} %stack.3), calls=%async_computation | async-start | bytes 1572864 | tf_op jit(solution)/shard_map/all_to_all | solution.py:64
Sparse Core Ops, SparseCore 0:
  21.1 60.8 all-gather.1
